TPU v7x, 32 devices: a whole 2x2x4 slice. The times are simulated.
32 devices in a mesh: clip: 2 (over y), tm: 8 (over z, x), tile: 2 (over core).
Axes of the slice: x: 2, y: 2, z: 4, core: 2. Of those that a mesh axis runs over, the one named last changes fastest.
Arguments:
- queries: bfloat16 [32, 256, 2048], P(('clip', 'tm'), 'tile'), parts along dimension 0, may hold values from -48 to 48
- keyvals: bfloat16 [2, 32, 256, 512], P(None, ('clip', 'tm'), 'tile'), parts along dimension 1, may hold values from -4 to 4
- proj_weight: bfloat16 [2048, 1024], P('tm', 'tile'), may hold values from -0.125 to 0.125
- norm_gain: float32 [1024], P('tile'), may hold values from 0.25 to 1.75
- frame_counts: int32 [32], P(('clip', 'tm')), parts along dimension 0, may hold values from 129 to 256, as said below
Outputs:
- dynamics: bfloat16 [32, 256, 1024], P(('clip', 'tm'), None, 'tile'), parts along dimension 0
There are 2 independent parts, one for each index of `clip`. A program takes and returns all parts, laid end to end along the dimension named above; an argument that names none is the same for every part. Nothing has to cross between parts.
Inputs may be any that keep to these rules, and one draw needn't show every extreme that they name: `frame_counts`: every spatial tile of every frame holds a live slot; some frame is full.
All inputs are finite; a program needn't handle non-finite values.
Results may differ from a plain program's by a relative error of at most 0.013.
Values may be sent and summed in bfloat16 or wider, within the bound.
No kernel may reach another device: no remote copies, remote signals or barrier semaphores. Data moves between devices by JAX's collectives and lax.ppermute only.
A program may use at most 64 MiB of HBM per device.

v0:
```python
import jax
import jax.numpy as jnp
from jax import lax
from jax.sharding import PartitionSpec as P

QHEADS = 16
KVHEADS = 4
HEAD_DIM = 128
IDM_DIM = 64
WINDOW = 4
PARTNER = 16


def passed_along(value, axis, steps):
    count = lax.axis_size(axis)
    initial, last = (max(0, -steps), min(count, count - steps))
    return lax.ppermute(value, axis, [(source, source + steps) for source in range(initial, last)])


def window_attention(query_block, key_block, value_block, live_keys, groups):
    row_count = query_block.shape[0]
    key_heads = key_block.shape[1]
    head_width = key_block.shape[2]
    grouped = query_block.reshape(row_count, key_heads, groups, head_width)
    scores = jnp.einsum(
        "ikgd,jkd->ikgj", grouped, key_block, preferred_element_type=jnp.float32
    ) * head_width ** (-0.5)
    key_mask = live_keys[None, None, None, :]
    row_max = jnp.max(jnp.where(key_mask, scores, -1e30), axis=-1, keepdims=True)
    weights = jnp.where(key_mask, jnp.exp(jnp.where(key_mask, scores, row_max) - row_max), 0.0)
    normalized = (weights / jnp.sum(weights, axis=-1, keepdims=True)).astype(jnp.bfloat16)
    blended = jnp.einsum(
        "ikgj,jkd->ikgd", normalized, value_block, preferred_element_type=jnp.float32
    )
    return blended.astype(jnp.bfloat16).reshape(row_count, key_heads * groups * head_width)


def normalize_heads(latent_block, gain):
    width = latent_block.shape[-1]
    heads = width // IDM_DIM
    values = latent_block.astype(jnp.float32).reshape(latent_block.shape[:-1] + (heads, IDM_DIM))
    scaled = values * lax.rsqrt(jnp.mean(values * values, axis=-1, keepdims=True) + 1e-06)
    scaled = scaled * gain.reshape(heads, IDM_DIM)
    return scaled.astype(jnp.bfloat16).reshape(latent_block.shape)


def local(queries, keyvals, proj_weight, norm_gain, frame_counts):
    frames_here = queries.shape[0]
    tile_tokens = queries.shape[1]
    groups = QHEADS // KVHEADS
    lead_frames = WINDOW - 1
    hop_total = (lead_frames + frames_here - 1) // frames_here
    tile_place = lax.axis_index("tile")
    received = []
    for hop_count in range(1, hop_total + 1):
        needed = min(frames_here, lead_frames - (hop_count - 1) * frames_here)
        piece_pair = passed_along(
            (keyvals[:, frames_here - needed :], frame_counts[frames_here - needed :]),
            "tm",
            hop_count,
        )
        received = [piece_pair] + received
    earlier_kv = jnp.concatenate([received_pair[0] for received_pair in received], axis=1)
    earlier_counts = jnp.concatenate([received_pair[1] for received_pair in received], axis=0)
    window_kv = jnp.concatenate([earlier_kv, keyvals], axis=1)
    window_counts = jnp.concatenate([earlier_counts, frame_counts], axis=0)
    slot_index = tile_place * tile_tokens + jnp.arange(tile_tokens, dtype=jnp.int32)
    attended_frames = []
    for frame_index in range(frames_here):
        block_kv = window_kv[:, frame_index : frame_index + WINDOW]
        live_keys = (
            slot_index[None, :] < window_counts[frame_index : frame_index + WINDOW, None]
        ).reshape(WINDOW * tile_tokens)
        key_block = block_kv[0].reshape(WINDOW * tile_tokens, KVHEADS, HEAD_DIM)
        value_block = block_kv[1].reshape(WINDOW * tile_tokens, KVHEADS, HEAD_DIM)
        attended_frames.append(
            window_attention(queries[frame_index], key_block, value_block, live_keys, groups)
        )
    attended = jnp.stack(attended_frames)
    query_width = attended.shape[2]
    full_columns = lax.all_gather(proj_weight, "tile", axis=1, tiled=True)
    token_rows = attended.reshape(frames_here * tile_tokens, query_width)
    summed = jnp.dot(
        token_rows,
        lax.all_gather(full_columns, "tm", axis=0, tiled=True),
        preferred_element_type=jnp.float32,
    )
    own_latent = summed.astype(jnp.bfloat16).reshape(
        frames_here, tile_tokens, full_columns.shape[1]
    )
    latent = lax.all_to_all(own_latent, "tile", split_axis=2, concat_axis=1, tiled=True)
    normed = normalize_heads(latent, norm_gain)
    frame_tokens = normed.shape[1]
    heads_here = normed.shape[2] // IDM_DIM
    distance = PARTNER // frames_here
    before_normed, before_counts = passed_along((normed, frame_counts), "tm", distance)
    after_normed, after_counts = passed_along((normed, frame_counts), "tm", -distance)
    slot_all = jnp.arange(frame_tokens, dtype=jnp.int32)
    results = []
    for frame_index in range(frames_here):
        key_rows = jnp.concatenate(
            [before_normed[frame_index], normed[frame_index], after_normed[frame_index]], axis=0
        )
        key_rows = key_rows.reshape(3 * frame_tokens, heads_here, IDM_DIM)
        live_keys = jnp.concatenate(
            [
                slot_all < before_counts[frame_index],
                slot_all < frame_counts[frame_index],
                slot_all < after_counts[frame_index],
            ]
        )
        query_rows = normed[frame_index].reshape(frame_tokens, heads_here, IDM_DIM)
        scores = jnp.einsum(
            "ihd,jhd->ihj", query_rows, key_rows, preferred_element_type=jnp.float32
        ) * IDM_DIM ** (-0.5)
        weights = jnp.where(live_keys[None, None, :], jnp.exp(scores), 0.0)
        normalized = (weights / jnp.sum(weights, axis=-1, keepdims=True)).astype(jnp.bfloat16)
        blended = jnp.einsum(
            "ihj,jhd->ihd", normalized, key_rows, preferred_element_type=jnp.float32
        )
        results.append(blended.astype(jnp.bfloat16).reshape(frame_tokens, heads_here * IDM_DIM))
    return jnp.stack(results)


def solution(mesh):
    in_specs = (
        P(("clip", "tm"), "tile", None),
        P(None, ("clip", "tm"), "tile", None),
        P("tm", "tile"),
        P("tile"),
        P(("clip", "tm")),
    )
    out_specs = P(("clip", "tm"), None, "tile")
    return jax.shard_map(local, mesh=mesh, in_specs=in_specs, out_specs=out_specs, check_vma=False)
```

profile of v0, /device:TPU:0, one launch (start us, length us, event | category | flops | bytes accessed | tf_op | source)
XLA Modules:
  0.0 124.8 jit_solution(14114580612585396030)
XLA Ops:
  6.5 4.3 %all_gather.6 = bf16[256,1024]{1,0:T(8,128)(2,1)} all-gather(bf16[256,512]{1,0:T(8,128)(2,1)} %param.7), channel_id=1, replica_groups=mesh['clip'=2,'tm'=8,'tile'=2] {'tile'}, dimensions={1}, use_global_device_ids=true | all-gather | bytes 786432 | tf_op jit(solution)/shard_map/all_gather | solution.py:81
  10.9 4.5 %collective-permute-start.3 = (s32[2]{0:T(128)}, s32[2]{0:T(128)S(1)}, u32[]{:S(2)}, u32[]{:S(2)}) collective-permute-start(s32[2]{0:T(128)} %param.9), channel_id=1, source_target_pairs={{0,2},{2,4},{4,6},{6,8},{8,10},{10,12},{12,14},{1,3},{3,5},{5,7},{... | collective-permute-start | bytes 32 | tf_op jit(solution)/shard_map/ppermute | solution.py:17
  15.4 0.7 collective-permute-start.5
  16.1 3.5 %collective-permute-start.1 = (bf16[2,2,128,512]{3,2,1,0:T(8,128)(2,1)}, bf16[2,2,128,512]{3,2,1,0:T(8,128)(2,1)S(1)}, u32[]{:S(2)}, u32[]{:S(2)}) collective-permute-start(bf16[2,2,128,512]{3,2,1,0:T(8,128)(2,1)} %param.6), channel_id=1, source_target_pairs={{0,2},{2,4},{4,6},{6,8},{8,10},{10,12},{12,14},{1,3},{3,5},{5,7},{... | collective-permute-start | bytes 1572872 | tf_op jit(solution)/shard_map/ppermute | solution.py:17
  19.6 1.0 slice.65
  20.6 3.5 %collective-permute-start = (bf16[2,1,128,512]{3,2,1,0:T(8,128)(2,1)S(1)}, bf16[2,1,128,512]{3,2,1,0:T(8,128)(2,1)S(1)}, u32[]{:S(2)}, u32[]{:S(2)}) collective-permute-start(bf16[2,1,128,512]{3,2,1,0:T(8,128)(2,1)S(1)} %slice.65), channel_id=1, source_target_pairs={{0,4},{2,6},{4,8},{6,10},{8,12},{10,14},{1,5},{3,7},{5,9},{7,11},{... | collective-permute-start | bytes 786440 | tf_op jit(solution)/shard_map/ppermute | solution.py:17
  24.0 1.4 %fusion.52 = (s32[1]{0:T(128)}, s32[1]{0:T(128)}) fusion(s32[2]{0:T(128)} %param.9), kind=kLoop, calls=%fused_computation.86 | loop fusion | bytes 16 | tf_op jit(solution)/shard_map/slice | solution.py:108
  25.4 4.0 %collective-permute-start.2 = (s32[1]{0:T(128)}, s32[1]{0:T(128)}, u32[]{:S(2)}, u32[]{:S(2)}) collective-permute-start(s32[1]{0:T(128)} %get-tuple-element.20), channel_id=1, source_target_pairs={{0,4},{2,6},{4,8},{6,10},{8,12},{10,14},{1,5},{3,7},{5,9},{7,11},{... | collective-permute-start | bytes 20 | tf_op jit(solution)/shard_map/ppermute | solution.py:17
  29.4 1.3 %fusion.49 = (bf16[1,128,2048]{2,1,0:T(8,128)(2,1)S(1)}, bf16[1,128,2048]{2,1,0:T(8,128)(2,1)S(1)}) fusion(bf16[2,128,2048]{2,1,0:T(8,128)(2,1)} %param.5), kind=kLoop, calls=%fused_computation.83 | loop fusion | bytes 2097152 | tf_op jit(solution)/shard_map/slice | solution.py:77
  30.7 0.3 copy.70
  31.0 0.3 copy.71
  31.4 0.6 iota_compare_fusion
  32.0 0.7 fusion.53
  32.7 0.7 iota_compare_fusion.1
  33.4 1.3 %iota_compare_fusion.2 = (pred[256]{0:T(512)(128)(4,1)S(1)}, pred[256]{0:T(512)(128)(4,1)S(1)}) fusion(s32[]{:T(128)} %bitcast.22, s32[]{:T(128)} %bitcast.21), kind=kLoop, calls=%fused_computation.65 | loop fusion | flops 512 | bytes 520 | tf_op jit(solution)/shard_map/lt | solution.py:108
  34.8 1.2 collective-permute-done.2
  36.0 0.8 pad_add_fusion.2
  37.1 0.2 fusion.48
  37.3 0.9 reshape_squeeze.21
  38.2 0.1 reshape.102
  38.3 1.8 %fusion.6 = (f32[128,4,4]{0,2,1:T(4,128)S(1)}, f32[4,512,128,4]{2,1,3,0:T(8,128)S(1)}) fusion(pred[512]{0:T(512)(128)(4,1)S(1)} %get-tuple-element.23, bf16[128,4,4,128]{0,3,2,1:T(8,128)(2,1)S(1)} %bitcast.120, bf16[512,4,128,1]{2,1,0,3:T(4,128)(2,1)} %bitcast.122), kind=kOutput, calls=%fused_computation.16 | convolution fusion | flops 271579136 | bytes 5251584 | tf_op jit(solution)/shard_map/ikgd,jkd->ikgj/dot_general | solution.py:25
  40.1 1.1 fusion.14
  41.2 1.4 %fusion.19 = bf16[4,128,128,4]{2,1,3,0:T(8,128)(2,1)S(1)} fusion(f32[4,512,128,4]{2,1,3,0:T(8,128)S(1)} %get-tuple-element.28, f32[128,4,4]{0,2,1:T(4,128)S(1)} %fusion.14, f32[128,4,4]{0,2,1:T(4,128)S(1)} %get-tuple-element.27, pred[512]{0:T(512)(128)(4,1)S(1)} %get-tuple-element.23, bf16[512,4,128,1]{2,1,0,3:T(4,128)(2,1)S(1)} %bitcast.125), kind=kOutput, calls=%fused_computation.29 | convolution fusion | flops 274989056 | bytes 5259776 | tf_op jit(solution)/shard_map/ikgj,jkd->ikgd/dot_general | solution.py:32
  42.6 0.2 copy.42
  42.9 0.1 reshape_squeeze.24
  43.0 0.1 reshape.103
  43.1 0.8 fusion.2
  43.9 1.1 fusion.15
  45.0 1.4 %fusion.18 = bf16[4,128,128,4]{2,1,3,0:T(8,128)(2,1)S(1)} fusion(f32[4,512,128,4]{2,1,3,0:T(8,128)S(1)} %get-tuple-element.26, f32[128,4,4]{0,2,1:T(4,128)S(1)} %fusion.15, f32[128,4,4]{0,2,1:T(4,128)S(1)} %get-tuple-element.25, pred[512]{0:T(512)(128)(4,1)S(1)} %get-tuple-element.24, bf16[512,4,128,1]{2,1,0,3:T(4,128)(2,1)S(1)} %bitcast.124), kind=kOutput, calls=%fused_computation.28 | convolution fusion | flops 274989056 | bytes 5259776 | tf_op jit(solution)/shard_map/ikgj,jkd->ikgd/dot_general | solution.py:32
  46.4 0.2 copy.43
  46.7 52.3 %all-gather.2.cloned.1.call-done = bf16[2048,1024]{1,0:T(8,128)(2,1)} async-done(((bf16[256,1024]{1,0:T(8,128)(2,1)}), bf16[2048,1024]{1,0:T(8,128)(2,1)}) %all-gather.2.cloned.1.call-update) | async-done | bytes 4194320 | tf_op jit(solution)/shard_map/all_gather | solution.py:85
  99.0 3.5 %convolution_convert_fusion = bf16[256,1024]{1,0:T(8,128)(2,1)S(1)} fusion(bf16[256,2048]{1,0:T(8,128)(2,1)S(1)} %bitcast.123, bf16[2048,1024]{1,0:T(8,128)(2,1)} %all-gather.2.cloned.1.call-done), kind=kOutput, calls=%fused_computation.30 | convolution fusion | flops 1074003968 | bytes 5767168 | tf_op jit(solution)/shard_map/dot_general | solution.py:83
  102.5 0.4 copy.44
  102.9 4.2 %all_to_all.4 = bf16[2,128,1024]{1,0,2:T(2,128)(2,1)S(1)} all-to-all(bf16[2,128,1024]{1,0,2:T(2,128)(2,1)S(1)} %copy.44), channel_id=1, replica_groups=mesh['clip'=2,'tm'=8,'tile'=2] {'tile'}, dimensions={2} | all-to-all | bytes 1048576 | tf_op jit(solution)/shard_map/all_to_all | solution.py:91
  107.1 0.5 copy.85
  107.6 0.8 reshape.95
  108.5 0.8 reshape.94
  109.3 0.1 multiply_reduce_fusion
  109.4 0.2 fusion.27
  109.6 0.7 collective-permute-start.4
  110.3 0.2 multiply_convert_fusion
  110.6 1.6 %bitcast_reduce_fusion.1 = (f32[256,8]{0,1:T(8,128)S(1)}, f32[8,768,256]{2,1,0:T(8,128)S(1)}) fusion(pred[768]{0:T(1024)(128)(4,1)S(1)} %pad_add_fusion, bf16[256,8,64]{0,2,1:T(8,128)(2,1)S(1)} %get-tuple-element.13, bf16[256,8,64]{0,2,1:T(8,128)(2,1)S(1)} %bitcast.133), kind=kOutput, calls=%fused_computation.4 | convolution fusion | flops 208402432 | bytes 6824704 | tf_op jit(solution)/shard_map/ihd,jhd->ihj/dot_general | solution.py:113
  112.3 1.5 %fusion.23 = bf16[8,64,256]{2,1,0:T(8,128)(2,1)S(1)} fusion(f32[8,768,256]{2,1,0:T(8,128)S(1)} %get-tuple-element.32, f32[256,8]{0,1:T(8,128)S(1)} %get-tuple-element.31, pred[768]{0:T(1024)(128)(4,1)S(1)} %pad_add_fusion, bf16[256,8,64]{0,2,1:T(8,128)(2,1)S(1)} %bitcast.134, bf16[256,8,64]{0,2,1:T(8,128)(2,1)S(1)} %get-tuple-element.13), kind=kOutput, calls=%fused_computation.32 | convolution fusion | flops 210108416 | bytes 7086848 | tf_op jit(solution)/shard_map/ihj,jhd->ihd/dot_general | solution.py:118
  113.7 0.1 copy.48
  113.9 1.6 %bitcast_reduce_fusion = (f32[256,8]{0,1:T(8,128)S(1)}, f32[8,768,256]{2,1,0:T(8,128)S(1)}) fusion(pred[768]{0:T(1024)(128)(4,1)S(1)} %pad_add_fusion.1, bf16[256,8,64]{0,2,1:T(8,128)(2,1)S(1)} %get-tuple-element.14, bf16[256,8,64]{0,2,1:T(8,128)(2,1)S(1)} %bitcast.131), kind=kOutput, calls=%fused_computation.1 | convolution fusion | flops 208402432 | bytes 6824704 | tf_op jit(solution)/shard_map/ihd,jhd->ihj/dot_general | solution.py:113
  115.5 1.5 %fusion.20 = bf16[8,64,256]{2,1,0:T(8,128)(2,1)S(1)} fusion(f32[8,768,256]{2,1,0:T(8,128)S(1)} %get-tuple-element.30, f32[256,8]{0,1:T(8,128)S(1)} %get-tuple-element.29, pred[768]{0:T(1024)(128)(4,1)S(1)} %pad_add_fusion.1, bf16[256,8,64]{0,2,1:T(8,128)(2,1)S(1)} %bitcast.132, bf16[256,8,64]{0,2,1:T(8,128)(2,1)S(1)} %get-tuple-element.14), kind=kOutput, calls=%fused_computation.31 | convolution fusion | flops 210108416 | bytes 7086848 | tf_op jit(solution)/shard_map/ihj,jhd->ihd/dot_general | solution.py:118
  117.0 0.1 copy.49
  117.1 0.8 pad_maximum_fusion.7
  (26 shorter events, 0.7 us)
Async XLA Ops:
  6.5 28.2 %copy-start.2 = (s32[2]{0:T(128)S(1)}, s32[2]{0:T(128)}, u32[]{:S(2)}) copy-start(s32[2]{0:T(128)} %param.9) | copy-start | bytes 28
  6.5 30.4 %copy-start = (bf16[2,2,128,512]{3,2,1,0:T(8,128)(2,1)S(1)}, bf16[2,2,128,512]{3,2,1,0:T(8,128)(2,1)}, u32[]{:S(2)}) copy-start(bf16[2,2,128,512]{3,2,1,0:T(8,128)(2,1)} %param.6) | copy-start | bytes 1572868
  6.5 24.8 %copy-start.1 = (f32[512]{0:T(512)S(1)}, f32[512]{0:T(512)}, u32[]{:S(2)}) copy-start(f32[512]{0:T(512)} %param.8) | copy-start | bytes 6148
  6.5 92.5 %all-gather.2.cloned.1.call-start = ((), (), s32[]{:S(2)}) async-start(), calls=%async_computation.1 | async-start | bytes 4718592 | tf_op jit(solution)/shard_map/all_gather | solution.py:85
  10.9 23.8 %collective-permute-start.3 = (s32[2]{0:T(128)}, s32[2]{0:T(128)S(1)}, u32[]{:S(2)}, u32[]{:S(2)}) collective-permute-start(s32[2]{0:T(128)} %param.9), channel_id=1, source_target_pairs={{0,2},{2,4},{4,6},{6,8},{8,10},{10,12},{12,14},{1,3},{3,5},{5,7},{... | collective-permute-start | bytes 32 | tf_op jit(solution)/shard_map/ppermute | solution.py:17
  15.4 16.6 %collective-permute-start.5 = (s32[2]{0:T(128)}, s32[2]{0:T(128)S(1)}, u32[]{:S(2)}, u32[]{:S(2)}) collective-permute-start(s32[2]{0:T(128)} %param.9), channel_id=1, source_target_pairs={} | collective-permute-start | bytes 32 | tf_op jit(solution)/shard_map/ppermute | solution.py:17
  16.1 20.8 %collective-permute-start.1 = (bf16[2,2,128,512]{3,2,1,0:T(8,128)(2,1)}, bf16[2,2,128,512]{3,2,1,0:T(8,128)(2,1)S(1)}, u32[]{:S(2)}, u32[]{:S(2)}) collective-permute-start(bf16[2,2,128,512]{3,2,1,0:T(8,128)(2,1)} %param.6), channel_id=1, source_target_pairs={{0,2},{2,4},{4,6},{6,8},{8,10},{10,12},{12,14},{1,3},{3,5},{5,7},{... | collective-permute-start | bytes 1572872 | tf_op jit(solution)/shard_map/ppermute | solution.py:17
  20.6 16.3 %collective-permute-start = (bf16[2,1,128,512]{3,2,1,0:T(8,128)(2,1)S(1)}, bf16[2,1,128,512]{3,2,1,0:T(8,128)(2,1)S(1)}, u32[]{:S(2)}, u32[]{:S(2)}) collective-permute-start(bf16[2,1,128,512]{3,2,1,0:T(8,128)(2,1)S(1)} %slice.65), channel_id=1, source_target_pairs={{0,4},{2,6},{4,8},{6,10},{8,12},{10,14},{1,5},{3,7},{5,9},{7,11},{... | collective-permute-start | bytes 786440 | tf_op jit(solution)/shard_map/ppermute | solution.py:17
  25.4 10.6 %collective-permute-start.2 = (s32[1]{0:T(128)}, s32[1]{0:T(128)}, u32[]{:S(2)}, u32[]{:S(2)}) collective-permute-start(s32[1]{0:T(128)} %get-tuple-element.20), channel_id=1, source_target_pairs={{0,4},{2,6},{4,8},{6,10},{8,12},{10,14},{1,5},{3,7},{5,9},{7,11},{... | collective-permute-start | bytes 20 | tf_op jit(solution)/shard_map/ppermute | solution.py:17
  109.6 0.9 collective-permute-start.4
Sparse Core Ops, SparseCore 0:
  11.0 87.9 all-gather.1
where the time goes:
time: 125 us
  waiting for transfers between devices  53.5 us (43%)
  starting transfers between devices  16.8 us (13%)
  matrix products  15.1 us (12%)
  between operations  13.8 us (11%)
  local copies, waits for them, and re-layouts  10 us (8%)
  blocking collectives  8.49 us (7%)
  other arithmetic  7.11 us (6%)
    all_gather x1, waiting for transfers between devices, local(): lax.all_gather(full_columns, 'tm', axis=0, tiled=True)  52.3 us
    ppermute x6, starting transfers between devices, passed_along(): lax.ppermute(value, axis, [(source, source + steps) for source in range(i...  16.8 us
    all_gather x1, blocking collectives, local(): full_columns = lax.all_gather(proj_weight, 'tile', axis=1, tiled=True)  4.34 us
    all_to_all x1, blocking collectives, local(): lax.all_to_all(own_latent, 'tile', split_axis=2, concat_axis=1, tiled=True)  4.15 us
    dot_general x1, matrix products, local(): jnp.dot(token_rows, lax.all_gather(full_columns, 'tm', axis=0, tiled=True...  3.49 us
    dot_general x2, matrix products, local(): jnp.einsum('ihd,jhd->ihj', query_rows, key_rows, preferred_element_type=j...  3.23 us
    dot_general x2, matrix products, local(): jnp.einsum('ihj,jhd->ihd', normalized, key_rows, preferred_element_type=j...  2.96 us
    dot_general x2, matrix products, window_attention(): jnp.einsum('ikgj,jkd->ikgd', normalized, value_block, preferred_element_t...  2.82 us
  transfers between devices with their start and end apart: 7, of which 2 were waited for; matrix products, arithmetic and copies ran while one was open for 15% of the time, Pallas kernels for 0%

commit v1 on v0

--- a/solution.py
+++ b/solution.py
@@ -9,6 +9,28 @@
 IDM_DIM = 64
 WINDOW = 4
 PARTNER = 16
+
+
+def in_order(tiles, dim):
+    tiles = jnp.moveaxis(tiles, 0, dim)
+    lengths = tiles.shape
+    return tiles.reshape(*lengths[:dim], lengths[dim] * lengths[dim + 1], *lengths[dim + 2 :])
+
+
+def gather_around(x, axis, dim):
+    count = lax.axis_size(axis)
+    pairs = [(i, (i + 1) % count) for i in range(count)]
+    back = [(b, a) for a, b in pairs]
+    lower, upper = ([], [])
+    for step in range(count - 1):
+        if step % 2 == 0:
+            lower.append(lax.ppermute(lower[-1] if lower else x, axis, pairs))
+        else:
+            upper.append(lax.ppermute(upper[-1] if upper else x, axis, back))
+    pieces = jnp.stack([*lower[::-1], x, *upper])
+    shift = lax.axis_index(axis) - len(lower)
+    pieces = pieces[(jnp.arange(count) - shift) % count]
+    return in_order(pieces, dim)
 
 
 def passed_along(value, axis, steps):
@@ -81,9 +103,7 @@
     full_columns = lax.all_gather(proj_weight, "tile", axis=1, tiled=True)
     token_rows = attended.reshape(frames_here * tile_tokens, query_width)
     summed = jnp.dot(
-        token_rows,
-        lax.all_gather(full_columns, "tm", axis=0, tiled=True),
-        preferred_element_type=jnp.float32,
+        token_rows, gather_around(full_columns, "tm", 0), preferred_element_type=jnp.float32
     )
     own_latent = summed.astype(jnp.bfloat16).reshape(
         frames_here, tile_tokens, full_columns.shape[1]

time: 125 us -> 149 us (1.19)
  starting transfers between devices: 16.8 us -> 40.5 us
  local copies, waits for them, and re-layouts: 10 us -> 28.6 us
  between operations: 13.8 us -> 0.44 us
  waiting for transfers between devices: 53.5 us -> 40.9 us
  matrix products: 15.1 us -> 19.7 us
  other arithmetic: 7.11 us -> 11.4 us
  blocking collectives: 8.49 us -> 6.53 us
    all_gather x1 -> x0, waiting for transfers between devices: 52.3 us -> none  [local(): lax.all_gather(full_columns, 'tm', axis=0, tiled=True)]
    ppermute x0 -> x7, waiting for transfers between devices: none -> 28.8 us  [the longest x4 28.4 us: gather_around(): lower.append(lax.ppermute(lower[-1] if lower else x, axis, pairs))]
    ppermute x0 -> x7, starting transfers between devices: none -> 25.4 us  [the longest x3 21.2 us: gather_around(): upper.append(lax.ppermute(upper[-1] if upper else x, axis, back))]
    unnamed x10 -> x23, local copies, waits for them, and re-layouts: 0.68 us -> 11.8 us
    ppermute x6, waiting for transfers between devices: 1.24 us -> 12.1 us  [passed_along(): lax.ppermute(value, axis, [(source, source + steps) for source in range(i...]
    gather x0 -> x1, local copies, waits for them, and re-layouts: none -> 4.96 us  [gather_around(): pieces = pieces[(jnp.arange(count) - shift) % count]]
    reduce_sum x2, other arithmetic: 2.14 us -> 6.65 us  [window_attention(): jnp.sum(weights, axis=-1, keepdims=True)]
    dot_general x2, matrix products: 2.59 us -> 6.46 us  [window_attention(): jnp.einsum('ikgd,jkd->ikgj', grouped, key_block, preferred_element_type=j...]
  transfers between devices with their start and end apart: 7 -> 13, of which waited for: 2 -> 5; matrix products, arithmetic and copies ran while one was open for 15% -> 27% of each run, Pallas kernels for 0% -> 0%
where the time goes in v1:
time: 149 us; the launch traced here: 148 us
  waiting for transfers between devices  40.9 us (27%)
  starting transfers between devices  40.5 us (27%)
  local copies, waits for them, and re-layouts  28.6 us (19%)
  matrix products  19.7 us (13%)
  other arithmetic  11.4 us (8%)
  blocking collectives  6.53 us (4%)
    ppermute x4, waiting for transfers between devices, gather_around(): lower.append(lax.ppermute(lower[-1] if lower else x, axis, pairs))  28.4 us
    ppermute x3, starting transfers between devices, gather_around(): upper.append(lax.ppermute(upper[-1] if upper else x, axis, back))  21.2 us
    ppermute x6, starting transfers between devices, passed_along(): lax.ppermute(value, axis, [(source, source + steps) for source in range(i...  15.1 us
    ppermute x6, waiting for transfers between devices, passed_along(): lax.ppermute(value, axis, [(source, source + steps) for source in range(i...  12.1 us
    unnamed x23, local copies, waits for them, and re-layouts  11.8 us
    reduce_sum x2, other arithmetic, window_attention(): jnp.sum(weights, axis=-1, keepdims=True)  6.65 us
    dot_general x2, matrix products, window_attention(): jnp.einsum('ikgd,jkd->ikgj', grouped, key_block, preferred_element_type=j...  6.46 us
    gather x1, local copies, waits for them, and re-layouts, gather_around(): pieces = pieces[(jnp.arange(count) - shift) % count]  4.96 us
  transfers between devices with their start and end apart: 13, of which 5 were waited for; matrix products, arithmetic and copies ran while one was open for 27% of the time, Pallas kernels for 0%

profile of v1, /device:TPU:0, one launch (start us, length us, event | category | flops | bytes accessed | tf_op | source)
XLA Modules:
  0.0 148.2 jit_solution(4093792330601904988)
XLA Ops:
  0.0 5.0 %collective-permute-start.3 = (s32[2]{0:T(128)}, s32[2]{0:T(128)S(1)}, u32[]{:S(2)}, u32[]{:S(2)}) collective-permute-start(s32[2]{0:T(128)} %param.9), channel_id=1, source_target_pairs={{0,2},{2,4},{4,6},{6,8},{8,10},{10,12},{12,14},{1,3},{3,5},{5,7},{... | collective-permute-start | bytes 32 | tf_op jit(solution)/shard_map/ppermute | solution.py:39
  5.0 0.7 collective-permute-start.12
  5.7 3.5 %collective-permute-start.1 = (bf16[2,2,128,512]{3,2,1,0:T(8,128)(2,1)}, bf16[2,2,128,512]{3,2,1,0:T(8,128)(2,1)S(1)}, u32[]{:S(2)}, u32[]{:S(2)}) collective-permute-start(bf16[2,2,128,512]{3,2,1,0:T(8,128)(2,1)} %param.6), channel_id=1, source_target_pairs={{0,2},{2,4},{4,6},{6,8},{8,10},{10,12},{12,14},{1,3},{3,5},{5,7},{... | collective-permute-start | bytes 1572872 | tf_op jit(solution)/shard_map/ppermute | solution.py:39
  9.2 1.3 fusion.54
  10.5 4.0 %collective-permute-start.2 = (s32[1]{0:T(128)}, s32[1]{0:T(128)}, u32[]{:S(2)}, u32[]{:S(2)}) collective-permute-start(s32[1]{0:T(128)} %get-tuple-element.20), channel_id=1, source_target_pairs={{0,4},{2,6},{4,8},{6,10},{8,12},{10,14},{1,5},{3,7},{5,9},{7,11},{... | collective-permute-start | bytes 20 | tf_op jit(solution)/shard_map/ppermute | solution.py:39
  14.5 2.4 %all_gather.3 = bf16[256,1024]{1,0:T(8,128)(2,1)S(1)} all-gather(bf16[256,512]{1,0:T(8,128)(2,1)} %param.7), channel_id=1, replica_groups=mesh['clip'=2,'tm'=8,'tile'=2] {'tile'}, dimensions={1}, use_global_device_ids=true | all-gather | bytes 786432 | tf_op jit(solution)/shard_map/all_gather | solution.py:103
  16.9 1.5 %collective-permute-start.4 = (bf16[256,1024]{1,0:T(8,128)(2,1)S(1)}, bf16[256,1024]{1,0:T(8,128)(2,1)}, u32[]{:S(2)}, u32[]{:S(2)}) collective-permute-start(bf16[256,1024]{1,0:T(8,128)(2,1)S(1)} %all_gather.3), channel_id=1, source_target_pairs={{0,2},{2,4},{4,6},{6,8},{8,10},{10,12},{12,14},{14,0},{1,3},{3,5},... | collective-permute-start | bytes 1572872 | tf_op jit(solution)/shard_map/ppermute | solution.py:27
  18.4 1.0 slice.65
  19.3 1.3 fusion.51
  21.9 3.3 %collective-permute-start.8 = (bf16[256,1024]{1,0:T(8,128)(2,1)S(1)}, bf16[256,1024]{1,0:T(8,128)(2,1)}, u32[]{:S(2)}, u32[]{:S(2)}) collective-permute-start(bf16[256,1024]{1,0:T(8,128)(2,1)S(1)} %all_gather.3), channel_id=1, source_target_pairs={{2,0},{4,2},{6,4},{8,6},{10,8},{12,10},{14,12},{0,14},{3,1},{5,3},... | collective-permute-start | bytes 1572872 | tf_op jit(solution)/shard_map/ppermute | solution.py:29
  25.2 0.6 fusion.55
  26.4 1.3 iota_compare_fusion.2
  27.8 1.3 collective-permute-start
  29.2 0.7 pad_add_fusion.2
  29.9 12.1 %collective-permute-done = bf16[2,1,128,512]{3,2,1,0:T(8,128)(2,1)S(1)} collective-permute-done((bf16[2,1,128,512]{3,2,1,0:T(8,128)(2,1)S(1)}, bf16[2,1,128,512]{3,2,1,0:T(8,128)(2,1)S(1)}, u32[]{:S(2)}, u32[]{:S(2)}) %collective-permute-start) | collective-permute-done | bytes 262176 | tf_op jit(solution)/shard_map/ppermute | solution.py:39
  42.3 0.9 fusion.50
  43.2 2.0 %reshape_squeeze.21 = bf16[512,4,128]{2,1,0:T(4,128)(2,1)} reshape(bf16[1,4,128,512]{3,2,1,0:T(8,128)(2,1)} %get-tuple-element.6) | data formatting | bytes 1048576 | tf_op jit(solution)/shard_map/reshape;squeeze | solution.py:96
  45.2 3.7 %fusion.6 = (f32[128,4,4]{0,2,1:T(4,128)S(1)}, f32[4,512,128,4]{2,1,3,0:T(8,128)}) fusion(pred[512]{0:T(512)(128)(4,1)S(1)} %get-tuple-element.23, bf16[128,4,4,128]{0,3,2,1:T(8,128)(2,1)S(1)} %bitcast.140, bf16[512,4,128,1]{2,1,0,3:T(4,128)(2,1)} %bitcast.142), kind=kOutput, calls=%fused_computation.17 | convolution fusion | flops 271579136 | bytes 5251584 | tf_op jit(solution)/shard_map/ikgd,jkd->ikgj/dot_general | solution.py:47
  49.1 3.4 %fusion.14 = f32[128,4,4]{0,2,1:T(4,128)S(1)} fusion(f32[4,512,128,4]{2,1,3,0:T(8,128)} %get-tuple-element.28, f32[128,4,4]{0,2,1:T(4,128)S(1)} %get-tuple-element.27, pred[512]{0:T(512)(128)(4,1)S(1)} %get-tuple-element.23), kind=kLoop, calls=%fused_computation.25 | loop fusion | flops 5240832 | bytes 4211200 | tf_op jit(solution)/shard_map/reduce_sum | solution.py:53
  52.6 2.2 %fusion.19 = bf16[4,128,128,4]{2,1,3,0:T(8,128)(2,1)} fusion(f32[4,512,128,4]{2,1,3,0:T(8,128)S(1)} %copy-done.1, f32[128,4,4]{0,2,1:T(4,128)S(1)} %fusion.14, f32[128,4,4]{0,2,1:T(4,128)S(1)} %get-tuple-element.27, pred[512]{0:T(512)(128)(4,1)S(1)} %get-tuple-element.23, bf16[512,4,128,1]{2,1,0,3:T(4,128)(2,1)S(1)} %bitcast.146), kind=kOutput, calls=%fused_computation.30 | convolution fusion | flops 274989056 | bytes 5259776 | tf_op jit(solution)/shard_map/ikgj,jkd->ikgd/dot_general | solution.py:54
  54.9 13.4 %collective-permute-done.5 = bf16[256,1024]{1,0:T(8,128)(2,1)S(1)} collective-permute-done((bf16[256,1024]{1,0:T(8,128)(2,1)}, bf16[256,1024]{1,0:T(8,128)(2,1)S(1)}, u32[]{:S(2)}, u32[]{:S(2)}) %collective-permute-start.5) | collective-permute-done | bytes 524320 | tf_op jit(solution)/shard_map/ppermute | solution.py:27
  68.3 2.7 %fusion.2 = (f32[128,4,4]{0,2,1:T(4,128)S(1)}, f32[4,512,128,4]{2,1,3,0:T(8,128)}) fusion(pred[512]{0:T(512)(128)(4,1)S(1)} %get-tuple-element.24, bf16[128,4,4,128]{0,3,2,1:T(8,128)(2,1)S(1)} %bitcast.139, bf16[512,4,128,1]{2,1,0,3:T(4,128)(2,1)S(1)} %bitcast.141), kind=kOutput, calls=%fused_computation.11 | convolution fusion | flops 271579136 | bytes 5251584 | tf_op jit(solution)/shard_map/ikgd,jkd->ikgj/dot_general | solution.py:47
  71.2 4.8 %collective-permute-start.9 = (bf16[256,1024]{1,0:T(8,128)(2,1)}, bf16[256,1024]{1,0:T(8,128)(2,1)}, u32[]{:S(2)}, u32[]{:S(2)}) collective-permute-start(bf16[256,1024]{1,0:T(8,128)(2,1)} %collective-permute-done.8), channel_id=1, source_target_pairs={{2,0},{4,2},{6,4},{8,6},{10,8},{12,10},{14,12},{0,14},{3,1},{5,3},... | collective-permute-start | bytes 1572872 | tf_op jit(solution)/shard_map/ppermute | solution.py:29
  75.9 3.2 %fusion.15 = f32[128,4,4]{0,2,1:T(4,128)S(1)} fusion(f32[4,512,128,4]{2,1,3,0:T(8,128)} %get-tuple-element.26, f32[128,4,4]{0,2,1:T(4,128)S(1)} %get-tuple-element.25, pred[512]{0:T(512)(128)(4,1)S(1)} %get-tuple-element.24), kind=kLoop, calls=%fused_computation.26 | loop fusion | flops 5240832 | bytes 4211200 | tf_op jit(solution)/shard_map/reduce_sum | solution.py:53
  79.2 10.1 %collective-permute-done.6 = bf16[256,1024]{1,0:T(8,128)(2,1)} collective-permute-done((bf16[256,1024]{1,0:T(8,128)(2,1)S(1)}, bf16[256,1024]{1,0:T(8,128)(2,1)}, u32[]{:S(2)}, u32[]{:S(2)}) %collective-permute-start.6) | collective-permute-done | bytes 524320 | tf_op jit(solution)/shard_map/ppermute | solution.py:27
  89.3 2.6 %collective-permute-start.7 = (bf16[256,1024]{1,0:T(8,128)(2,1)}, bf16[256,1024]{1,0:T(8,128)(2,1)}, u32[]{:S(2)}, u32[]{:S(2)}) collective-permute-start(bf16[256,1024]{1,0:T(8,128)(2,1)} %collective-permute-done.6), channel_id=1, source_target_pairs={{0,2},{2,4},{4,6},{6,8},{8,10},{10,12},{12,14},{14,0},{1,3},{3,5},... | collective-permute-start | bytes 1572872 | tf_op jit(solution)/shard_map/ppermute | solution.py:27
  91.9 1.4 fusion.18
  94.3 13.2 %collective-permute-start.10 = (bf16[256,1024]{1,0:T(8,128)(2,1)}, bf16[256,1024]{1,0:T(8,128)(2,1)S(1)}, u32[]{:S(2)}, u32[]{:S(2)}) collective-permute-start(bf16[256,1024]{1,0:T(8,128)(2,1)} %collective-permute-done.9), channel_id=1, source_target_pairs={{2,0},{4,2},{6,4},{8,6},{10,8},{12,10},{14,12},{0,14},{3,1},{5,3},... | collective-permute-start | bytes 1572872 | tf_op jit(solution)/shard_map/ppermute | solution.py:29
  107.5 4.9 %collective-permute-done.7 = bf16[256,1024]{1,0:T(8,128)(2,1)} collective-permute-done((bf16[256,1024]{1,0:T(8,128)(2,1)}, bf16[256,1024]{1,0:T(8,128)(2,1)}, u32[]{:S(2)}, u32[]{:S(2)}) %collective-permute-start.7) | collective-permute-done | bytes 524320 | tf_op jit(solution)/shard_map/ppermute | solution.py:27
  112.4 1.9 %bitcast_dynamic-update-slice_fusion.7 = bf16[8,256,1024]{2,1,0:T(8,128)(2,1)} fusion(bf16[256,1024]{1,0:T(8,128)(2,1)} %collective-permute-done.7), kind=kLoop, calls=%fused_computation.53 | loop fusion | bytes 1048576
  114.2 1.9 %bitcast_dynamic-update-slice_fusion.6 = bf16[8,256,1024]{2,1,0:T(8,128)(2,1)} fusion(bf16[8,256,1024]{2,1,0:T(8,128)(2,1)} %bitcast_dynamic-update-slice_fusion.7, bf16[256,1024]{1,0:T(8,128)(2,1)} %collective-permute-done.6), kind=kLoop, calls=%fused_computation.52 | loop fusion | bytes 1048576
  116.1 0.8 bitcast_dynamic-update-slice_fusion.5
  117.0 1.9 %bitcast_dynamic-update-slice_fusion.4 = bf16[8,256,1024]{2,1,0:T(8,128)(2,1)} fusion(bf16[8,256,1024]{2,1,0:T(8,128)(2,1)} %bitcast_dynamic-update-slice_fusion.5, bf16[256,1024]{1,0:T(8,128)(2,1)} %collective-permute-done.4), kind=kLoop, calls=%fused_computation.50 | loop fusion | bytes 1048576
  118.8 0.8 bitcast_dynamic-update-slice_fusion.3
  119.7 1.9 %bitcast_dynamic-update-slice_fusion.2 = bf16[8,256,1024]{2,1,0:T(8,128)(2,1)} fusion(bf16[8,256,1024]{2,1,0:T(8,128)(2,1)} %bitcast_dynamic-update-slice_fusion.3, bf16[256,1024]{1,0:T(8,128)(2,1)} %collective-permute-done.8), kind=kLoop, calls=%fused_computation.48 | loop fusion | bytes 1048576
  121.6 1.9 %bitcast_dynamic-update-slice_fusion.1 = bf16[8,256,1024]{2,1,0:T(8,128)(2,1)} fusion(bf16[8,256,1024]{2,1,0:T(8,128)(2,1)} %bitcast_dynamic-update-slice_fusion.2, bf16[256,1024]{1,0:T(8,128)(2,1)} %collective-permute-done.9), kind=kLoop, calls=%fused_computation.47 | loop fusion | bytes 1048576
  123.5 0.8 bitcast_dynamic-update-slice_fusion
  124.3 5.0 %gather_fusion = bf16[8,256,1024]{2,1,0:T(8,128)(2,1)} fusion(bf16[8,256,1024]{2,1,0:T(8,128)(2,1)} %bitcast_dynamic-update-slice_fusion, s32[1024]{0:T(1024)S(1)} %pad_clamp_fusion), kind=kCustom, calls=%fused_computation | custom fusion | bytes 8388640 | tf_op jit(solution)/shard_map/gather | solution.py:32
  129.3 3.4 %convolution_convert_fusion = bf16[256,1024]{1,0:T(8,128)(2,1)S(1)} fusion(bf16[256,2048]{1,0:T(8,128)(2,1)S(1)} %bitcast.143, bf16[2048,1024]{1,0:T(8,128)(2,1)} %bitcast.137), kind=kOutput, calls=%fused_computation.31 | convolution fusion | flops 1074003968 | bytes 5767168 | tf_op jit(solution)/shard_map/dot_general | solution.py:105
  133.1 4.2 %all_to_all.4 = bf16[2,128,1024]{1,0,2:T(2,128)(2,1)S(1)} all-to-all(bf16[2,128,1024]{1,0,2:T(2,128)(2,1)S(1)} %copy.44), channel_id=1, replica_groups=mesh['clip'=2,'tm'=8,'tile'=2] {'tile'}, dimensions={2} | all-to-all | bytes 1048576 | tf_op jit(solution)/shard_map/all_to_all | solution.py:111
  137.8 0.8 reshape.148
  138.7 0.8 reshape.147
  139.8 0.7 collective-permute-start.11
  140.8 1.6 %bitcast_reduce_fusion.1 = (f32[256,8]{0,1:T(8,128)S(1)}, f32[8,768,256]{2,1,0:T(8,128)S(1)}) fusion(pred[768]{0:T(1024)(128)(4,1)S(1)} %pad_add_fusion, bf16[256,8,64]{0,2,1:T(8,128)(2,1)S(1)} %get-tuple-element.13, bf16[256,8,64]{0,2,1:T(8,128)(2,1)S(1)} %bitcast.153), kind=kOutput, calls=%fused_computation.5 | convolution fusion | flops 208402432 | bytes 6824704 | tf_op jit(solution)/shard_map/ihd,jhd->ihj/dot_general | solution.py:133
  142.4 1.5 fusion.23
  144.1 1.6 %bitcast_reduce_fusion = (f32[256,8]{0,1:T(8,128)S(1)}, f32[8,768,256]{2,1,0:T(8,128)S(1)}) fusion(pred[768]{0:T(1024)(128)(4,1)S(1)} %pad_add_fusion.1, bf16[256,8,64]{0,2,1:T(8,128)(2,1)S(1)} %get-tuple-element.14, bf16[256,8,64]{0,2,1:T(8,128)(2,1)S(1)} %bitcast.151), kind=kOutput, calls=%fused_computation.2 | convolution fusion | flops 208402432 | bytes 6824704 | tf_op jit(solution)/shard_map/ihd,jhd->ihj/dot_general | solution.py:133
  145.7 1.5 %fusion.20 = bf16[8,64,256]{2,1,0:T(8,128)(2,1)S(1)} fusion(f32[8,768,256]{2,1,0:T(8,128)S(1)} %get-tuple-element.30, f32[256,8]{0,1:T(8,128)S(1)} %get-tuple-element.29, pred[768]{0:T(1024)(128)(4,1)S(1)} %pad_add_fusion.1, bf16[256,8,64]{0,2,1:T(8,128)(2,1)S(1)} %bitcast.152, bf16[256,8,64]{0,2,1:T(8,128)(2,1)S(1)} %get-tuple-element.14), kind=kOutput, calls=%fused_computation.32 | convolution fusion | flops 210108416 | bytes 7086848 | tf_op jit(solution)/shard_map/ihj,jhd->ihd/dot_general | solution.py:138
  147.3 0.8 pad_maximum_fusion.7
  (54 shorter events, 5.4 us)
Async XLA Ops:
  0.0 29.1 %copy-start.5 = (s32[2]{0:T(128)S(1)}, s32[2]{0:T(128)}, u32[]{:S(2)}) copy-start(s32[2]{0:T(128)} %param.9) | copy-start | bytes 28
  0.0 42.2 %copy-start.2 = (bf16[2,2,128,512]{3,2,1,0:T(8,128)(2,1)S(1)}, bf16[2,2,128,512]{3,2,1,0:T(8,128)(2,1)}, u32[]{:S(2)}) copy-start(bf16[2,2,128,512]{3,2,1,0:T(8,128)(2,1)} %param.6) | copy-start | bytes 1572868
  0.0 21.2 %copy-start.4 = (f32[512]{0:T(512)S(1)}, f32[512]{0:T(512)}, u32[]{:S(2)}) copy-start(f32[512]{0:T(512)} %param.8) | copy-start | bytes 6148
  0.0 27.7 %collective-permute-start.3 = (s32[2]{0:T(128)}, s32[2]{0:T(128)S(1)}, u32[]{:S(2)}, u32[]{:S(2)}) collective-permute-start(s32[2]{0:T(128)} %param.9), channel_id=1, source_target_pairs={{0,2},{2,4},{4,6},{6,8},{8,10},{10,12},{12,14},{1,3},{3,5},{5,7},{... | collective-permute-start | bytes 32 | tf_op jit(solution)/shard_map/ppermute | solution.py:39
  5.0 16.8 %collective-permute-start.12 = (s32[2]{0:T(128)}, s32[2]{0:T(128)S(1)}, u32[]{:S(2)}, u32[]{:S(2)}) collective-permute-start(s32[2]{0:T(128)} %param.9), channel_id=1, source_target_pairs={} | collective-permute-start | bytes 32 | tf_op jit(solution)/shard_map/ppermute | solution.py:39
  5.7 36.4 %collective-permute-start.1 = (bf16[2,2,128,512]{3,2,1,0:T(8,128)(2,1)}, bf16[2,2,128,512]{3,2,1,0:T(8,128)(2,1)S(1)}, u32[]{:S(2)}, u32[]{:S(2)}) collective-permute-start(bf16[2,2,128,512]{3,2,1,0:T(8,128)(2,1)} %param.6), channel_id=1, source_target_pairs={{0,2},{2,4},{4,6},{6,8},{8,10},{10,12},{12,14},{1,3},{3,5},{5,7},{... | collective-permute-start | bytes 1572872 | tf_op jit(solution)/shard_map/ppermute | solution.py:39
  10.5 18.7 %collective-permute-start.2 = (s32[1]{0:T(128)}, s32[1]{0:T(128)}, u32[]{:S(2)}, u32[]{:S(2)}) collective-permute-start(s32[1]{0:T(128)} %get-tuple-element.20), channel_id=1, source_target_pairs={{0,4},{2,6},{4,8},{6,10},{8,12},{10,14},{1,5},{3,7},{5,9},{7,11},{... | collective-permute-start | bytes 20 | tf_op jit(solution)/shard_map/ppermute | solution.py:39
  16.9 35.6 %collective-permute-start.4 = (bf16[256,1024]{1,0:T(8,128)(2,1)S(1)}, bf16[256,1024]{1,0:T(8,128)(2,1)}, u32[]{:S(2)}, u32[]{:S(2)}) collective-permute-start(bf16[256,1024]{1,0:T(8,128)(2,1)S(1)} %all_gather.3), channel_id=1, source_target_pairs={{0,2},{2,4},{4,6},{6,8},{8,10},{10,12},{12,14},{14,0},{1,3},{3,5},... | collective-permute-start | bytes 1572872 | tf_op jit(solution)/shard_map/ppermute | solution.py:27
  21.9 49.3 %collective-permute-start.8 = (bf16[256,1024]{1,0:T(8,128)(2,1)S(1)}, bf16[256,1024]{1,0:T(8,128)(2,1)}, u32[]{:S(2)}, u32[]{:S(2)}) collective-permute-start(bf16[256,1024]{1,0:T(8,128)(2,1)S(1)} %all_gather.3), channel_id=1, source_target_pairs={{2,0},{4,2},{6,4},{8,6},{10,8},{12,10},{14,12},{0,14},{3,1},{5,3},... | collective-permute-start | bytes 1572872 | tf_op jit(solution)/shard_map/ppermute | solution.py:29
  27.8 14.3 %collective-permute-start = (bf16[2,1,128,512]{3,2,1,0:T(8,128)(2,1)S(1)}, bf16[2,1,128,512]{3,2,1,0:T(8,128)(2,1)S(1)}, u32[]{:S(2)}, u32[]{:S(2)}) collective-permute-start(bf16[2,1,128,512]{3,2,1,0:T(8,128)(2,1)S(1)} %slice.65), channel_id=1, source_target_pairs={{0,4},{2,6},{4,8},{6,10},{8,12},{10,14},{1,5},{3,7},{5,9},{7,11},{... | collective-permute-start | bytes 786440 | tf_op jit(solution)/shard_map/ppermute | solution.py:39
  49.1 3.5 %copy-start.1 = (f32[4,512,128,4]{2,1,3,0:T(8,128)S(1)}, f32[4,512,128,4]{2,1,3,0:T(8,128)}, u32[]{:S(2)}) copy-start(f32[4,512,128,4]{2,1,3,0:T(8,128)} %get-tuple-element.28) | copy-start | bytes 12582916
  52.5 15.8 %collective-permute-start.5 = (bf16[256,1024]{1,0:T(8,128)(2,1)}, bf16[256,1024]{1,0:T(8,128)(2,1)S(1)}, u32[]{:S(2)}, u32[]{:S(2)}) collective-permute-start(bf16[256,1024]{1,0:T(8,128)(2,1)} %collective-permute-done.4), channel_id=1, source_target_pairs={{0,2},{2,4},{4,6},{6,8},{8,10},{10,12},{12,14},{14,0},{1,3},{3,5},... | collective-permute-start | bytes 1572872 | tf_op jit(solution)/shard_map/ppermute | solution.py:27
  68.3 21.0 %collective-permute-start.6 = (bf16[256,1024]{1,0:T(8,128)(2,1)S(1)}, bf16[256,1024]{1,0:T(8,128)(2,1)}, u32[]{:S(2)}, u32[]{:S(2)}) collective-permute-start(bf16[256,1024]{1,0:T(8,128)(2,1)S(1)} %collective-permute-done.5), channel_id=1, source_target_pairs={{0,2},{2,4},{4,6},{6,8},{8,10},{10,12},{12,14},{14,0},{1,3},{3,5},... | collective-permute-start | bytes 1572872 | tf_op jit(solution)/shard_map/ppermute | solution.py:27
  71.1 20.8 %copy-start = (f32[4,512,128,4]{2,1,3,0:T(8,128)S(1)}, f32[4,512,128,4]{2,1,3,0:T(8,128)}, u32[]{:S(2)}) copy-start(f32[4,512,128,4]{2,1,3,0:T(8,128)} %get-tuple-element.26) | copy-start | bytes 12582916
  71.2 23.1 %collective-permute-start.9 = (bf16[256,1024]{1,0:T(8,128)(2,1)}, bf16[256,1024]{1,0:T(8,128)(2,1)}, u32[]{:S(2)}, u32[]{:S(2)}) collective-permute-start(bf16[256,1024]{1,0:T(8,128)(2,1)} %collective-permute-done.8), channel_id=1, source_target_pairs={{2,0},{4,2},{6,4},{8,6},{10,8},{12,10},{14,12},{0,14},{3,1},{5,3},... | collective-permute-start | bytes 1572872 | tf_op jit(solution)/shard_map/ppermute | solution.py:29
  89.3 23.0 %collective-permute-start.7 = (bf16[256,1024]{1,0:T(8,128)(2,1)}, bf16[256,1024]{1,0:T(8,128)(2,1)}, u32[]{:S(2)}, u32[]{:S(2)}) collective-permute-start(bf16[256,1024]{1,0:T(8,128)(2,1)} %collective-permute-done.6), channel_id=1, source_target_pairs={{0,2},{2,4},{4,6},{6,8},{8,10},{10,12},{12,14},{14,0},{1,3},{3,5},... | collective-permute-start | bytes 1572872 | tf_op jit(solution)/shard_map/ppermute | solution.py:27
  91.9 1.4 copy-start.3
  94.3 29.2 %collective-permute-start.10 = (bf16[256,1024]{1,0:T(8,128)(2,1)}, bf16[256,1024]{1,0:T(8,128)(2,1)S(1)}, u32[]{:S(2)}, u32[]{:S(2)}) collective-permute-start(bf16[256,1024]{1,0:T(8,128)(2,1)} %collective-permute-done.9), channel_id=1, source_target_pairs={{2,0},{4,2},{6,4},{8,6},{10,8},{12,10},{14,12},{0,14},{3,1},{5,3},... | collective-permute-start | bytes 1572872 | tf_op jit(solution)/shard_map/ppermute | solution.py:29
  139.8 0.9 collective-permute-start.11
